TPU v7x, 32 devices: a whole 2x2x4 slice. The times are simulated.
32 devices in a mesh: row: 4 (over y, x), dict: 8 (over z, core).
Axes of the slice: x: 2, y: 2, z: 4, core: 2. Of those that a mesh axis runs over, the one named last changes fastest.
Arguments:
- activations: bfloat16 [4096, 4096], P(('row', 'dict')), may hold values from -6 to 6
- block_ids: int32 [4096, 4], P(('row', 'dict')), may hold values from 0 to 15, all different within a row; in each aligned block of 128 rows (0 to 127, 128 to 255, ...) at most 48 rows name the same one
- enc_weight: bfloat16 [2048, 4096], P('dict'), may hold values from -0.09375 to 0.09375
- enc_bias: float32 [2048], P('dict'), may hold values from -3 to 3
- dec_weight: bfloat16 [2048, 4096], P('dict'), may hold values from -0.25 to 0.25
- dec_bias: float32 [4096], replicated, may hold values from -3 to 3
Outputs:
- rebuilt: bfloat16 [4096, 4096], P(('row', 'dict'))
- enc_grad: bfloat16 [4096, 2048], P('row', 'dict')
- dec_grad: bfloat16 [4096, 2048], P('row', 'dict')
Inputs may be any that keep to these rules, and one draw needn't show every extreme that they name: `block_ids`: each row names 4 different blocks. Among the rows of one device no block is named by more than 48 rows, and some block is named by exactly 48.
All inputs are finite; a program needn't handle non-finite values.
Results may differ from a plain program's by a relative error of at most 0.0059.
Values may be sent and summed in bfloat16 or wider, within the bound.
A program may use at most 128 MiB of HBM per device.

v0:
```python
import jax
import jax.numpy as jnp
from jax import lax
from jax.sharding import PartitionSpec as P

BS = 128
K = 4


LOSS_SCALE = 0.03125


def gelu_tanh(values):
    return jax.nn.gelu(values, approximate=True)


def gelu_grad(pre_act, upstream):
    return jax.vjp(gelu_tanh, pre_act)[1](upstream)[0]


def slot_plan(block_ids, groups, total_blocks, slot_depth):
    rows_total = block_ids.shape[0]
    picks = block_ids.shape[1]
    per_group = rows_total // groups
    flat_ids = block_ids.reshape(groups, per_group * picks)
    onehot = (
        flat_ids[:, :, None] == jnp.arange(total_blocks, dtype=jnp.int32)[None, None, :]
    ).astype(jnp.int32)
    rank_in_block = jnp.sum((jnp.cumsum(onehot, axis=1) - 1) * onehot, axis=2)
    group_index = jnp.arange(groups, dtype=jnp.int32)[:, None]
    target = ((flat_ids * groups + group_index) * slot_depth + rank_in_block).reshape(-1)
    source_row = jnp.arange(rows_total * picks, dtype=jnp.int32) // picks
    filled = (
        jnp.full((total_blocks * groups * slot_depth,), rows_total, jnp.int32)
        .at[target]
        .set(source_row)
    )
    return (target, filled)


def pack_rows(values, filled, shape):
    padded = jnp.concatenate([values, jnp.zeros((1, values.shape[1]), values.dtype)], axis=0)
    return padded[filled].reshape(shape)


def on_device(activations, block_ids, enc_weight, enc_bias, dec_weight, dec_bias):
    rows_here, features = activations.shape
    dict_size = lax.axis_size("dict")
    row_size = lax.axis_size("row")
    local_latents = enc_weight.shape[0]
    block_count = local_latents // BS
    total_blocks = block_count * dict_size
    slot_depth = max(2, 3 * rows_here * K // (2 * total_blocks))
    enc_blocks = enc_weight.reshape(block_count, BS, features)
    dec_blocks = dec_weight.reshape(block_count, BS, features)
    bias_blocks = enc_bias.reshape(block_count, BS)
    shifted = (activations.astype(jnp.float32) - dec_bias[None, :]).astype(jnp.bfloat16)
    target, filled = slot_plan(block_ids, 1, total_blocks, slot_depth)
    outgoing = pack_rows(shifted, filled, (dict_size, block_count, slot_depth, features))
    encode_received = lax.all_to_all(outgoing, "dict", split_axis=0, concat_axis=0, tiled=True)
    pre_act = jnp.einsum(
        "sbmd,bcd->sbmc", encode_received, enc_blocks, preferred_element_type=jnp.float32
    )
    pre_act = pre_act + bias_blocks[None, :, None, :]
    encode_latent = gelu_tanh(pre_act).astype(jnp.bfloat16)
    partial_value = jnp.einsum(
        "sbmc,bcd->sbmd", encode_latent, dec_blocks, preferred_element_type=jnp.float32
    ).astype(jnp.bfloat16)
    partial_value, pre_act, latent, received = (
        partial_value,
        pre_act,
        encode_latent,
        encode_received,
    )
    returned = lax.all_to_all(partial_value, "dict", split_axis=0, concat_axis=0, tiled=True)
    slot_parts = (
        returned.reshape(-1, features)[target].astype(jnp.float32).reshape(rows_here, K, features)
    )
    recon_full = dec_bias[None, :] + jnp.sum(slot_parts, axis=1)
    rebuilt = recon_full.astype(jnp.bfloat16)
    residual = ((recon_full - activations.astype(jnp.float32)) * LOSS_SCALE).astype(jnp.bfloat16)
    residual_sent = pack_rows(residual, filled, (dict_size, block_count, slot_depth, features))
    residual_held = lax.all_to_all(residual_sent, "dict", split_axis=0, concat_axis=0, tiled=True)
    upstream = jnp.einsum(
        "sbmd,bcd->sbmc", residual_held, dec_blocks, preferred_element_type=jnp.float32
    )
    latent_grad = gelu_grad(pre_act, upstream).astype(jnp.bfloat16)
    product = jnp.einsum(
        "sbmc,sbmd->dbc", latent, residual_held, preferred_element_type=jnp.float32
    )
    dec_grad = lax.psum_scatter(
        product.reshape(features // row_size * lax.axis_size("row"), local_latents),
        "row",
        scatter_dimension=0,
        tiled=True,
    ).astype(jnp.bfloat16)
    product = jnp.einsum(
        "sbmc,sbmd->dbc", latent_grad, received, preferred_element_type=jnp.float32
    )
    enc_grad = lax.psum_scatter(
        product.reshape(features // row_size * lax.axis_size("row"), local_latents),
        "row",
        scatter_dimension=0,
        tiled=True,
    ).astype(jnp.bfloat16)
    return (rebuilt, enc_grad, dec_grad)


def solution(mesh):
    return jax.shard_map(
        on_device,
        mesh=mesh,
        in_specs=(
            P(("row", "dict"), None),
            P(("row", "dict"), None),
            P("dict", None),
            P("dict"),
            P("dict", None),
            P(),
        ),
        out_specs=(P(("row", "dict"), None), P("row", "dict"), P("row", "dict")),
        check_vma=False,
    )
```

profile of v0, /device:TPU:0, one launch (start us, length us, event | category | flops | bytes accessed | tf_op | source)
XLA Modules:
  0.0 625.9 jit_solution(16201291888327313781)
XLA Ops:
  7.2 0.0 copy-start
  7.2 0.8 broadcast_multiply_fusion
  8.0 0.8 copy.22
  8.8 0.1 eq.27
  9.0 1.2 reduce-window.6
  10.1 0.2 slice_reduce_fusion
  10.4 0.1 copy.21
  10.5 0.1 mul.77
  10.6 0.1 copy.25
  10.7 0.1 broadcast.122
  10.8 0.1 fusion.30
  10.9 2.4 scatter_custom_fusion
  13.4 1.4 fusion.5
  14.8 0.1 concatenate.6
  14.9 5.7 gather_fusion
  20.6 145.6 %all_to_all.15 = bf16[8,2,48,4096]{3,2,1,0:T(8,128)(2,1)S(1)} all-to-all(bf16[8,2,48,4096]{3,2,1,0:T(8,128)(2,1)} %bitcast.56), channel_id=1, replica_groups=mesh['row'=4,'dict'=8] {'dict'}, dimensions={0} | all-to-all | bytes 12582912 | tf_op jit(solution)/shard_map/all_to_all | solution.py:60
  166.2 0.0 copy-done.5
  166.2 0.0 copy-done.6
  166.2 2.8 multiply_convert_fusion
  169.0 0.0 copy-done.1
  169.0 0.0 copy-done
  169.0 1.8 fusion.4
  170.8 3.0 copy.27
  173.8 4.8 all-to-all-start.1
  178.6 0.2 reduce-scatter.5.cloned.1.call-start
  178.8 138.7 %all-to-all-done.1 = bf16[8,2,48,4096]{3,2,1,0:T(8,128)(2,1)} async-done(((bf16[8,2,48,4096]{3,2,1,0:T(8,128)(2,1)}), bf16[8,2,48,4096]{3,2,1,0:T(8,128)(2,1)}, u32[]{:S(2)}, u32[]{:S(2)}) %all-to-all-start.1) | async-done | bytes 6291488 | tf_op jit(solution)/shard_map/all_to_all | solution.py:75
  317.5 12.2 %gather_fusion.1 = bf16[512,4096]{1,0:T(8,128)(2,1)} fusion(bf16[768,4096]{1,0:T(8,128)(2,1)} %bitcast.18, s32[1024]{0:T(1024)S(1)} %pad_clamp_fusion), kind=kCustom, calls=%fused_computation.1 | custom fusion | bytes 8390656 | tf_op jit(solution)/shard_map/gather | solution.py:77
  329.8 8.3 %reshape.200 = f32[128,4,4096]{2,1,0:T(4,128)} reshape(bf16[512,4096]{1,0:T(8,128)(2,1)} %gather_fusion.1) | data formatting | bytes 12582912 | tf_op jit(solution)/shard_map/convert_element_type | solution.py:77
  338.1 10.1 %reduce_sum.22 = f32[128,4096]{1,0:T(8,128)} reduce(f32[128,4,4096]{2,1,0:T(4,128)} %reshape.200, f32[]{:T(128)} %constant.49.clone.1), dimensions={1}, to_apply=%region_4.5 | reduce | flops 1572864 | bytes 10485764 | tf_op jit(solution)/shard_map/reduce_sum | solution.py:79
  348.2 0.0 copy-done.3
  348.2 2.9 fusion.7
  351.1 0.1 concatenate.7
  351.2 5.7 gather_fusion.2
  356.9 143.0 %all_to_all.16 = bf16[8,2,48,4096]{3,2,1,0:T(8,128)(2,1)S(1)} all-to-all(bf16[8,2,48,4096]{3,2,1,0:T(8,128)(2,1)} %bitcast.55), channel_id=1, replica_groups=mesh['row'=4,'dict'=8] {'dict'}, dimensions={0} | all-to-all | bytes 12582912 | tf_op jit(solution)/shard_map/all_to_all | solution.py:83
  499.9 3.8 fusion.26
  503.7 0.1 copy-done.2
  503.8 5.6 copy.32
  509.4 0.0 reduce-scatter.5.cloned.1.call-update
  509.4 0.0 reduce-scatter.3.cloned.1.call-start
  509.5 0.9 copy-done.7
  510.4 4.7 fusion.23
  515.1 6.2 fusion.28
  521.2 5.7 copy.30
  527.0 0.0 reduce-scatter.3.cloned.1.call-update
  527.0 34.0 %reduce-scatter.5.cloned.1.call-done = f32[1024,256]{1,0:T(8,128)} async-done(((f32[4096,256]{1,0:T(8,128)}), f32[1024,256]{1,0:T(8,128)}) %reduce-scatter.5.cloned.1.call-update) | async-done | bytes 1048592 | tf_op jit(solution)/shard_map/reduce_scatter | solution.py:91
  561.0 2.1 convert_element_type.58
  563.1 53.9 %reduce-scatter.3.cloned.1.call-done = f32[1024,256]{1,0:T(8,128)} async-done(((f32[4096,256]{1,0:T(8,128)}), f32[1024,256]{1,0:T(8,128)}) %reduce-scatter.3.cloned.1.call-update) | async-done | bytes 1048592 | tf_op jit(solution)/shard_map/reduce_scatter | solution.py:100
  617.0 2.1 convert_element_type.57
  (18 shorter events, 0.1 us)
Async XLA Ops:
  7.2 161.8 %copy-start = (bf16[256,4096]{1,0:T(8,128)(2,1)S(1)}, bf16[256,4096]{1,0:T(8,128)(2,1)}, u32[]{:S(2)}) copy-start(bf16[256,4096]{1,0:T(8,128)(2,1)} %param.10) | copy-start | bytes 6291460
  20.6 145.6 %copy-start.5 = (bf16[256,4096]{1,0:T(8,128)(2,1)S(1)}, bf16[256,4096]{1,0:T(8,128)(2,1)}, u32[]{:S(2)}) copy-start(bf16[256,4096]{1,0:T(8,128)(2,1)} %param.8) | copy-start | bytes 6291460
  20.6 145.6 %copy-start.6 = (f32[256]{0:T(256)S(1)}, f32[256]{0:T(256)}, u32[]{:S(2)}) copy-start(f32[256]{0:T(256)} %param.9) | copy-start | bytes 3076
  166.2 2.8 copy-start.1
  173.8 143.7 %all-to-all-start.1 = ((bf16[8,2,48,4096]{3,2,1,0:T(8,128)(2,1)}), bf16[8,2,48,4096]{3,2,1,0:T(8,128)(2,1)}, u32[]{:S(2)}, u32[]{:S(2)}) async-start(bf16[8,2,48,4096]{3,2,1,0:T(8,128)(2,1)} %copy.27), calls=%async_computation.1 | async-start | bytes 12582912 | tf_op jit(solution)/shard_map/all_to_all | solution.py:75
  178.6 382.4 %reduce-scatter.5.cloned.1.call-start = ((), (), s32[]{:S(2)}) async-start(), calls=%async_computation.6 | async-start | bytes 5242880 | tf_op jit(solution)/shard_map/reduce_scatter | solution.py:91
  338.1 10.1 %copy-start.3 = (bf16[128,4096]{1,0:T(8,128)(2,1)S(1)}, bf16[128,4096]{1,0:T(8,128)(2,1)}, u32[]{:S(2)}) copy-start(bf16[128,4096]{1,0:T(8,128)(2,1)} %param.6) | copy-start | bytes 3145732
  338.1 10.1 %copy-start.4 = (f32[4096]{0:T(1024)S(1)}, f32[4096]{0:T(1024)}, u32[]{:S(2)}) copy-start(f32[4096]{0:T(1024)} %param.11) | copy-start | bytes 49156
  499.9 3.9 copy-start.2
  509.4 1.0 copy-start.7
  509.4 107.6 %reduce-scatter.3.cloned.1.call-start = ((), (), s32[]{:S(2)}) async-start(), calls=%async_computation.5 | async-start | bytes 5242880 | tf_op jit(solution)/shard_map/reduce_scatter | solution.py:100
Sparse Core Ops, SparseCore 0:
  509.5 51.4 reduce-scatter.4
  564.3 52.6 reduce-scatter.2
where the time goes:
time: 627 us; the launch traced here: 626 us
  blocking collectives  289 us (46%)
  waiting for transfers between devices  227 us (36%)
  local copies, waits for them, and re-layouts  51.5 us (8%)
  other arithmetic  20.8 us (3%)
  matrix products  19.2 us (3%)
  between operations  14.2 us (2%)
    all_to_all x1, blocking collectives, on_device(): lax.all_to_all(outgoing, 'dict', split_axis=0, concat_axis=0, tiled=True)  146 us
    all_to_all x1, blocking collectives, on_device(): lax.all_to_all(residual_sent, 'dict', split_axis=0, concat_axis=0, tiled=...  143 us
    all_to_all x1, waiting for transfers between devices, on_device(): lax.all_to_all(partial_value, 'dict', split_axis=0, concat_axis=0, tiled=...  139 us
    reduce_scatter x2, waiting for transfers between devices, on_device(): lax.psum_scatter(product.reshape(features // row_size * lax.axis_size('ro...  87.9 us
  transfers between devices with their start and end apart: 3, of which 3 were waited for; matrix products, arithmetic and copies ran while one was open for 3% of the time, Pallas kernels for 0%

commit v1 on v0

--- a/solution.py
+++ b/solution.py
@@ -106,9 +106,65 @@
     return (rebuilt, enc_grad, dec_grad)
 
 
+def gelu_and_slope(values):
+    inner = 0.7978845608 * (values + 0.044715 * values * values * values)
+    bend = jnp.tanh(inner)
+    half = 0.5 * (1.0 + bend)
+    slope = half + 0.5 * values * (1.0 - bend * bend) * 0.7978845608 * (
+        1.0 + 3.0 * 0.044715 * values * values
+    )
+    return values * half, slope
+
+
+def dense_on_device(activations, block_ids, enc_weight, enc_bias, dec_weight, dec_bias):
+    local_latents = enc_weight.shape[0]
+    block_count = local_latents // BS
+    me = lax.axis_index("dict")
+    shifted = (activations.astype(jnp.float32) - dec_bias[None, :]).astype(jnp.bfloat16)
+    ids = lax.all_gather(block_ids, "dict", axis=0, tiled=True)
+    held = lax.all_gather(shifted, "dict", axis=0, tiled=True)
+    mine = me * block_count + jnp.arange(local_latents, dtype=jnp.int32) // BS
+    mask = jnp.any(ids[:, :, None] == mine[None, None, :], axis=1)
+    pre_act = lax.dot_general(
+        held, enc_weight, (((1,), (1,)), ((), ())), preferred_element_type=jnp.float32
+    )
+    pre_act = pre_act + enc_bias[None, :]
+    value, slope = gelu_and_slope(pre_act)
+    latent = jnp.where(mask, value, 0.0).astype(jnp.bfloat16)
+    slope = jnp.where(mask, slope, 0.0)
+    partial_sum = jnp.dot(latent, dec_weight, preferred_element_type=jnp.float32)
+    total = lax.psum_scatter(
+        partial_sum.astype(jnp.bfloat16), "dict", scatter_dimension=0, tiled=True
+    )
+    recon_full = dec_bias[None, :] + total.astype(jnp.float32)
+    rebuilt = recon_full.astype(jnp.bfloat16)
+    residual = ((recon_full - activations.astype(jnp.float32)) * LOSS_SCALE).astype(jnp.bfloat16)
+    residual_held = lax.all_gather(residual, "dict", axis=0, tiled=True)
+    upstream = lax.dot_general(
+        residual_held, dec_weight, (((1,), (1,)), ((), ())), preferred_element_type=jnp.float32
+    )
+    latent_grad = (slope * upstream).astype(jnp.bfloat16)
+
+    def reduced(rows_by_features, rows_by_latents):
+        product = lax.dot_general(
+            rows_by_features,
+            rows_by_latents,
+            (((0,), (0,)), ((), ())),
+            preferred_element_type=jnp.float32,
+        )
+        return lax.psum_scatter(product, "row", scatter_dimension=0, tiled=True).astype(
+            jnp.bfloat16
+        )
+
+    dec_grad = reduced(residual_held, latent)
+    enc_grad = reduced(held, latent_grad)
+    return (rebuilt, enc_grad, dec_grad)
+
+
 def solution(mesh):
+    few_blocks = mesh.shape["dict"] <= 8
     return jax.shard_map(
-        on_device,
+        dense_on_device if few_blocks else on_device,
         mesh=mesh,
         in_specs=(
             P(("row", "dict"), None),

time: 627 us -> 404 us (0.64)
  blocking collectives: 289 us -> 14.5 us
  waiting for transfers between devices: 227 us -> 325 us
  local copies, waits for them, and re-layouts: 51.5 us -> 1.94 us
  matrix products: 19.2 us -> 38 us
  other arithmetic: 20.8 us -> 10.7 us
    all_to_all x2 -> x0, blocking collectives: 289 us -> none  [the longest x1 146 us: on_device(): lax.all_to_all(outgoing, 'dict', split_axis=0, concat_axis=0, tiled=True)]
    all_gather x0 -> x2, waiting for transfers between devices: none -> 150 us  [the longest x1 80.5 us: dense_on_device(): residual_held = lax.all_gather(residual, 'dict', axis=0, tiled=True)]
    all_to_all x1 -> x0, waiting for transfers between devices: 139 us -> none  [on_device(): lax.all_to_all(partial_value, 'dict', split_axis=0, concat_axis=0, tiled=...]
    reduce_scatter x2 -> x3, waiting for transfers between devices: 87.9 us -> 175 us  [the longest x1 88.3 us: dense_on_device(): lax.psum_scatter(partial_sum.astype(jnp.bfloat16), 'dict', scatter_dimens...]
    gather x3 -> x0, local copies, waits for them, and re-layouts: 23.6 us -> none  [the longest x1 12.2 us: on_device(): returned.reshape(-1, features)[target].astype(jnp.float32)]
    dot_general x5 -> x4, matrix products: 19.2 us -> 38 us  [the longest x2 25.8 us: reduced(): lax.dot_general(rows_by_features, rows_by_latents, (((0,), (0,)), ((), ()...]
    all_gather x0 -> x1, blocking collectives: none -> 14.5 us  [dense_on_device(): ids = lax.all_gather(block_ids, 'dict', axis=0, tiled=True)]
    convert_element_type x2 -> x0, local copies, waits for them, and re-layouts: 11.4 us -> none  [the longest x1 8.33 us: on_device(): returned.reshape(-1, features)[target].astype(jnp.float32)]
  transfers between devices with their start and end apart: 3 -> 5, of which waited for: 3 -> 5; matrix products, arithmetic and copies ran while one was open for 3% -> 5% of each run, Pallas kernels for 0% -> 0%
where the time goes in v1:
time: 404 us
  waiting for transfers between devices  325 us (80%)
  matrix products  38 us (9%)
  blocking collectives  14.5 us (4%)
  between operations  13.8 us (3%)
  other arithmetic  10.7 us (3%)
    reduce_scatter x1, waiting for transfers between devices, dense_on_device(): lax.psum_scatter(partial_sum.astype(jnp.bfloat16), 'dict', scatter_dimens...  88.3 us
    reduce_scatter x2, waiting for transfers between devices, reduced(): lax.psum_scatter(product, 'row', scatter_dimension=0, tiled=True)  86.3 us
    all_gather x1, waiting for transfers between devices, dense_on_device(): residual_held = lax.all_gather(residual, 'dict', axis=0, tiled=True)  80.5 us
    all_gather x1, waiting for transfers between devices, dense_on_device(): held = lax.all_gather(shifted, 'dict', axis=0, tiled=True)  69.6 us
    dot_general x2, matrix products, reduced(): lax.dot_general(rows_by_features, rows_by_latents, (((0,), (0,)), ((), ()...  25.8 us
    all_gather x1, blocking collectives, dense_on_device(): ids = lax.all_gather(block_ids, 'dict', axis=0, tiled=True)  14.5 us
  transfers between devices with their start and end apart: 5, of which 5 were waited for; matrix products, arithmetic and copies ran while one was open for 5% of the time, Pallas kernels for 0%

profile of v1, /device:TPU:0, one launch (start us, length us, event | category | flops | bytes accessed | tf_op | source)
XLA Modules:
  0.0 404.1 jit_solution(12838851521415117076)
XLA Ops:
  7.2 0.0 copy-start
  7.2 0.0 all-gather.3.cloned.1.call-start
  7.2 2.5 fusion
  9.8 0.0 all-gather.3.cloned.1.call-update
  9.8 0.0 reduce-scatter.4.cloned.1.call-start
  9.8 14.5 %all_gather.9 = s32[1024,4]{0,1:T(4,128)S(1)} all-gather(s32[128,4]{0,1:T(4,128)} %param.7), channel_id=1, replica_groups=mesh['row'=4,'dict'=8] {'dict'}, dimensions={0}, use_global_device_ids=true | all-gather | bytes 18432 | tf_op jit(solution)/shard_map/all_gather | solution.py:124
  24.4 1.0 compare_reduce_fusion
  25.4 69.6 %all-gather.3.cloned.1.call-done = bf16[1024,4096]{1,0:T(8,128)(2,1)} async-done(((bf16[128,4096]{1,0:T(8,128)(2,1)}), bf16[1024,4096]{1,0:T(8,128)(2,1)}) %all-gather.3.cloned.1.call-update) | async-done | bytes 8388624 | tf_op jit(solution)/shard_map/all_gather | solution.py:125
  95.0 6.4 %convolution_add_fusion = f32[1024,256]{1,0:T(8,128)S(1)} fusion(bf16[1024,4096]{1,0:T(8,128)(2,1)} %all-gather.3.cloned.1.call-done, bf16[256,4096]{1,0:T(8,128)(2,1)} %param.8, f32[256]{0:T(256)} %param.9), kind=kOutput, calls=%fused_computation.12 | convolution fusion | flops 2147745792 | bytes 11535360 | tf_op jit(solution)/shard_map/dot_general | solution.py:128
  101.4 0.0 copy-start.2
  101.4 1.0 copy-done.2
  102.3 0.0 copy-done
  102.3 5.8 %convolution_convert_fusion = bf16[1024,4096]{1,0:T(8,128)(2,1)} fusion(bf16[256,4096]{1,0:T(8,128)(2,1)S(1)} %copy-done, pred[1024,256]{1,0:T(8,128)(4,1)S(1)} %compare_reduce_fusion, f32[1024,256]{1,0:T(8,128)S(1)} %convolution_add_fusion), kind=kOutput, calls=%fused_computation | convolution fusion | flops 2154299392 | bytes 11796480 | tf_op jit(solution)/shard_map/dot_general | solution.py:135
  108.1 0.0 copy-start.1
  108.1 0.0 copy-start.4
  108.1 0.0 reduce-scatter.4.cloned.1.call-update
  108.1 0.0 all-gather.5.cloned.1.call-start
  108.2 88.3 %reduce-scatter.4.cloned.1.call-done = bf16[128,4096]{1,0:T(8,128)(2,1)} async-done(((bf16[1024,4096]{1,0:T(8,128)(2,1)}), bf16[128,4096]{1,0:T(8,128)(2,1)}) %reduce-scatter.4.cloned.1.call-update) | async-done | bytes 1048592 | tf_op jit(solution)/shard_map/reduce_scatter | solution.py:136
  196.4 0.0 copy-done.1
  196.4 0.0 copy-done.4
  196.4 3.0 fusion.2
  199.5 0.0 all-gather.5.cloned.1.call-update
  199.5 0.0 reduce-scatter.8.cloned.1.call-start
  199.5 80.5 %all-gather.5.cloned.1.call-done = bf16[1024,4096]{1,0:T(8,128)(2,1)} async-done(((bf16[128,4096]{1,0:T(8,128)(2,1)}), bf16[1024,4096]{1,0:T(8,128)(2,1)}) %all-gather.5.cloned.1.call-update) | async-done | bytes 8388624 | tf_op jit(solution)/shard_map/all_gather | solution.py:142
  280.1 8.2 %fusion.12 = f32[4096,256]{1,0:T(8,128)} fusion(bf16[1024,4096]{1,0:T(8,128)(2,1)} %all-gather.5.cloned.1.call-done, pred[1024,256]{1,0:T(8,128)(4,1)S(1)} %compare_reduce_fusion, f32[1024,256]{1,0:T(8,128)} %copy-done.2), kind=kOutput, calls=%fused_computation.27 | convolution fusion | flops 2150105088 | bytes 13893632 | tf_op jit(solution)/shard_map/dot_general | solution.py:149
  288.2 0.0 copy-start.3
  288.2 0.0 reduce-scatter.8.cloned.1.call-update
  288.3 0.2 reduce-scatter.6.cloned.1.call-start
  288.5 1.0 copy-done.3
  289.5 17.6 %fusion.13 = f32[4096,256]{1,0:T(8,128)} fusion(bf16[1024,4096]{1,0:T(8,128)(2,1)} %all-gather.3.cloned.1.call-done, bf16[1024,4096]{1,0:T(8,128)(2,1)} %all-gather.5.cloned.1.call-done, bf16[256,4096]{1,0:T(8,128)(2,1)S(1)} %copy-done, pred[1024,256]{1,0:T(8,128)(4,1)S(1)} %compare_reduce_fusion, f32[1024,256]{1,0:T(8,128)S(1)} %copy-done.3), kind=kOutput, calls=%fused_computation.28 | convolution fusion | flops 4300210176 | bytes 24379392 | tf_op jit(solution)/shard_map/dot_general | solution.py:149
  307.1 0.0 reduce-scatter.6.cloned.1.call-update
  307.1 32.5 %reduce-scatter.8.cloned.1.call-done = f32[1024,256]{1,0:T(8,128)} async-done(((f32[4096,256]{1,0:T(8,128)}), f32[1024,256]{1,0:T(8,128)}) %reduce-scatter.8.cloned.1.call-update) | async-done | bytes 1048592 | tf_op jit(solution)/shard_map/reduce_scatter | solution.py:155
  339.6 2.1 convert_element_type.40
  341.7 53.8 %reduce-scatter.6.cloned.1.call-done = f32[1024,256]{1,0:T(8,128)} async-done(((f32[4096,256]{1,0:T(8,128)}), f32[1024,256]{1,0:T(8,128)}) %reduce-scatter.6.cloned.1.call-update) | async-done | bytes 1048592 | tf_op jit(solution)/shard_map/reduce_scatter | solution.py:155
  395.5 2.1 convert_element_type.39
  (1 shorter events, 0.0 us)
Async XLA Ops:
  7.2 95.2 %copy-start = (bf16[256,4096]{1,0:T(8,128)(2,1)S(1)}, bf16[256,4096]{1,0:T(8,128)(2,1)}, u32[]{:S(2)}) copy-start(bf16[256,4096]{1,0:T(8,128)(2,1)} %param.10) | copy-start | bytes 6291460
  7.2 87.8 %all-gather.3.cloned.1.call-start = ((), (), s32[]{:S(2)}) async-start(), calls=%async_computation.3 | async-start | bytes 9437184 | tf_op jit(solution)/shard_map/all_gather | solution.py:125
  9.8 186.6 %reduce-scatter.4.cloned.1.call-start = ((), (), s32[]{:S(2)}) async-start(), calls=%async_computation.4 | async-start | bytes 9437184 | tf_op jit(solution)/shard_map/reduce_scatter | solution.py:136
  101.4 1.0 copy-start.2
  108.1 88.3 %copy-start.1 = (bf16[128,4096]{1,0:T(8,128)(2,1)S(1)}, bf16[128,4096]{1,0:T(8,128)(2,1)}, u32[]{:S(2)}) copy-start(bf16[128,4096]{1,0:T(8,128)(2,1)} %param.6) | copy-start | bytes 3145732
  108.1 88.3 %copy-start.4 = (f32[4096]{0:T(1024)S(1)}, f32[4096]{0:T(1024)}, u32[]{:S(2)}) copy-start(f32[4096]{0:T(1024)} %param.11) | copy-start | bytes 49156
  108.1 171.9 %all-gather.5.cloned.1.call-start = ((), (), s32[]{:S(2)}) async-start(), calls=%async_computation.5 | async-start | bytes 9437184 | tf_op jit(solution)/shard_map/all_gather | solution.py:142
  199.5 140.1 %reduce-scatter.8.cloned.1.call-start = ((), (), s32[]{:S(2)}) async-start(), calls=%async_computation.7 | async-start | bytes 5242880 | tf_op jit(solution)/shard_map/reduce_scatter | solution.py:155
  288.2 1.2 copy-start.3
  288.3 107.2 %reduce-scatter.6.cloned.1.call-start = ((), (), s32[]{:S(2)}) async-start(), calls=%async_computation.6 | async-start | bytes 5242880 | tf_op jit(solution)/shard_map/reduce_scatter | solution.py:155
Sparse Core Ops, SparseCore 0:
  10.2 84.7 all-gather.2
  108.2 88.1 reduce-scatter.3
  199.6 80.3 all-gather.4
  288.4 51.2 reduce-scatter.7
  342.7 52.6 reduce-scatter.5

commit v2 on v0

--- a/solution.py
+++ b/solution.py
@@ -1,6 +1,8 @@
 import jax
 import jax.numpy as jnp
 from jax import lax
+from jax.experimental import pallas as pl
+from jax.experimental.pallas import tpu as pltpu
 from jax.sharding import PartitionSpec as P
 
 BS = 128
@@ -106,9 +108,403 @@
     return (rebuilt, enc_grad, dec_grad)
 
 
+def gelu_and_slope(values):
+    inner = 0.7978845608 * (values + 0.044715 * values * values * values)
+    bend = jnp.tanh(inner)
+    half = 0.5 * (1.0 + bend)
+    slope = half + 0.5 * values * (1.0 - bend * bend) * 0.7978845608 * (
+        1.0 + 3.0 * 0.044715 * values * values
+    )
+    return values * half, slope
+
+
+SUBS = 4
+
+
+def step_kernel(
+    x_ref, act_ref, bias_ref, dbias_ref, enc_ref, dec_ref,
+    rebuilt_ref, enc_grad_ref, dec_grad_ref,
+    held, res, enc_far, dec_far, bias_far, part, total, incoming, latent, slope,
+    acc, fin, near_out, near_in, row_out, row_in,
+    w_send, w_recv, x_send, x_recv, p_send, p_recv, r_send, r_recv,
+    n_send, n_recv, g_send, g_recv,
+):
+    rows, features = act_ref.shape
+    row = lax.axis_index("row")
+    dict_at = lax.axis_index("dict")
+    row_size = lax.axis_size("row")
+    places = lax.axis_size("dict") // 2
+    place = dict_at // 2
+    core = dict_at % 2
+    far = place * 2 + (1 - core)
+    sub = rows // SUBS
+    half = enc_ref.shape[0]
+    slab = features // row_size
+    f32, bf16 = jnp.float32, jnp.bfloat16
+
+    def along(step):
+        return (row, dict_at + 2 * step)
+
+    def remote(src, dst, send, recv, device):
+        return pltpu.make_async_remote_copy(
+            src_ref=src, dst_ref=dst, send_sem=send, recv_sem=recv,
+            device_id=device, device_id_type=pl.DeviceIdType.MESH,
+        )
+
+    barrier = pltpu.get_barrier_semaphore()
+
+    def greet(device):
+        pl.semaphore_signal(
+            barrier, inc=1, device_id=device, device_id_type=pl.DeviceIdType.MESH
+        )
+
+    greet((row, far))
+    for k in range(1, row_size):
+        greet(((row + k) % row_size, dict_at))
+
+    @pl.when(place > 0)
+    def _():
+        greet(along(-1))
+
+    @pl.when(place < places - 1)
+    def _():
+        greet(along(1))
+
+    inside = jnp.logical_and(place > 0, place < places - 1)
+
+    @pl.when(inside)
+    def _():
+        pl.semaphore_wait(barrier, row_size + 2)
+
+    @pl.when(jnp.logical_not(inside))
+    def _():
+        pl.semaphore_wait(barrier, row_size + 1)
+
+    def part_rows(s):
+        return pl.ds(pl.multiple_of(s * sub, sub), sub)
+
+    def has_next(way):
+        return jnp.logical_and(place + way >= 0, place + way < places)
+
+    def x_copy(q, s, way, own):
+        src = x_ref.at[part_rows(s)] if own else held.at[q, part_rows(s)]
+        return remote(
+            src, held.at[q, part_rows(s)], x_send.at[(way + 1) // 2, q, s],
+            x_recv.at[q, s], along(way),
+        )
+
+    def r_copy(q, s, way):
+        return remote(
+            res.at[q, part_rows(s)], res.at[q, part_rows(s)],
+            r_send.at[(way + 1) // 2, q, s], r_recv.at[q, s], along(way),
+        )
+
+    def p_copy(q, s, way):
+        return remote(
+            part.at[q, part_rows(s)], incoming.at[(way + 1) // 2, q, part_rows(s)],
+            p_send.at[q, s], p_recv.at[(way + 1) // 2, q, s], along(way),
+        )
+
+    for s in range(SUBS):
+        for way in (1, -1):
+            @pl.when(has_next(way))
+            def _():
+                x_copy(place, s, way, True).start()
+
+    weights = [
+        remote(src, dst, w_send.at[i], w_recv.at[i], (row, far))
+        for i, (src, dst) in enumerate(
+            ((bias_ref, bias_far), (enc_ref, enc_far), (dec_ref, dec_far))
+        )
+    ]
+    for copy in weights:
+        copy.start()
+    held[place] = x_ref[...]
+    for copy in weights:
+        copy.wait_recv()
+
+    def forward(q):
+        data = held[q, :, :features]
+        active = held[q, :, features:]
+        block = lax.broadcasted_iota(jnp.int32, (active.shape[1], half), 0)
+        column = lax.broadcasted_iota(jnp.int32, (active.shape[1], half), 1)
+        blocks = half // BS
+        for h, (weight, bias, owner) in enumerate(
+            ((enc_ref, bias_ref, dict_at), (enc_far, bias_far, far))
+        ):
+            chosen = jnp.where(block == owner * blocks + column // BS, 1.0, 0.0).astype(bf16)
+            mask = jnp.dot(active, chosen, preferred_element_type=f32) > 0.5
+            pre = lax.dot_general(
+                data, weight[...], (((1,), (1,)), ((), ())), preferred_element_type=f32
+            )
+            value, bend = gelu_and_slope(pre + bias[0:1, :])
+            latent[q, :, h * half : (h + 1) * half] = jnp.where(mask, value, 0.0).astype(bf16)
+            slope[q, :, h * half : (h + 1) * half] = jnp.where(mask, bend, 0.0)
+
+    def decoded(q, columns):
+        return jnp.dot(
+            latent[q, :, :half], dec_ref[:, columns], preferred_element_type=f32
+        ) + jnp.dot(latent[q, :, half:], dec_far[:, columns], preferred_element_type=f32)
+
+    wide = 1024
+
+    def each_columns(body):
+        @pl.loop(0, features // wide)
+        def _(i):
+            body(pl.ds(pl.multiple_of(i * wide, wide), wide))
+
+    forward(place)
+
+    def keep_total(columns):
+        total[:, columns] = decoded(place, columns) + dbias_ref[:, columns]
+
+    each_columns(keep_total)
+
+    @pl.loop(2, 2 * places)
+    def _(i):
+        way = 1 - 2 * (i % 2)
+        q = place - way * (i // 2)
+
+        @pl.when(jnp.logical_and(q >= 0, q < places))
+        def _():
+            @pl.loop(0, SUBS)
+            def _(s):
+                x_copy(q, s, way, False).wait_recv()
+
+                @pl.when(has_next(way))
+                def _():
+                    x_copy(q, s, way, False).start()
+
+            forward(q)
+
+            def keep_part(columns):
+                part[q, :, columns] = decoded(q, columns).astype(bf16)
+
+            each_columns(keep_part)
+
+            @pl.when(jnp.logical_not(has_next(way)))
+            def _():
+                @pl.loop(0, SUBS)
+                def _(s):
+                    p_copy(q, s, -way).start()
+
+    def finish(s):
+        here = part_rows(s)
+        full = total[here, :]
+        rebuilt_ref[here, :] = full.astype(bf16)
+        res[place, here, :] = ((full - act_ref[here, :].astype(f32)) * LOSS_SCALE).astype(bf16)
+        for way in (1, -1):
+            @pl.when(has_next(way))
+            def _():
+                r_copy(place, s, way).start()
+
+    @pl.loop(0, 2)
+    def _(turn):
+        low = jnp.where(place < places // 2, 1, -1)
+        way = low * (1 - 2 * turn)
+        lane = (way + 1) // 2
+
+        @pl.when(has_next(-way))
+        def _():
+            @pl.loop(0, places)
+            def _(t):
+                q = place + way * t
+
+                @pl.when(jnp.logical_and(q >= 0, q < places))
+                def _():
+                    @pl.loop(0, SUBS)
+                    def _(s):
+                        here = part_rows(s)
+                        p_copy(q, s, way).wait_recv()
+
+                        @pl.when(t == 0)
+                        def _():
+                            total[here, :] += incoming[lane, q, here, :].astype(f32)
+
+                            @pl.when(turn == 1)
+                            def _():
+                                finish(s)
+
+                        @pl.when(t > 0)
+                        def _():
+                            part[q, here, :] = (
+                                part[q, here, :].astype(f32)
+                                + incoming[lane, q, here, :].astype(f32)
+                            ).astype(bf16)
+                            p_copy(q, s, way).start()
+
+    def backward(q):
+        for h, weight in enumerate((dec_ref, dec_far)):
+            span = slice(h * half, (h + 1) * half)
+            up = lax.dot_general(
+                res[q], weight[...], (((1,), (1,)), ((), ())), preferred_element_type=f32
+            )
+            slope[q, :, span] = slope[q, :, span] * up
+
+    backward(place)
+
+    @pl.loop(2, 2 * places)
+    def _(i):
+        way = 1 - 2 * (i % 2)
+        q = place - way * (i // 2)
+
+        @pl.when(jnp.logical_and(q >= 0, q < places))
+        def _():
+            @pl.loop(0, SUBS)
+            def _(s):
+                r_copy(q, s, way).wait_recv()
+
+                @pl.when(has_next(way))
+                def _():
+                    r_copy(q, s, way).start()
+
+            backward(q)
+
+    tile = 256
+
+    def near_copy(g, k):
+        return remote(
+            near_out.at[g, k], near_in.at[g, k], n_send.at[g, k], n_recv.at[g, k], (row, far)
+        )
+
+    def row_copy(g, k):
+        return remote(
+            row_out.at[g, k], row_in.at[g, k], g_send.at[g, k], g_recv.at[g, k],
+            ((row + k + 1) % row_size, dict_at),
+        )
+
+    for g, left in enumerate((res, held)):
+        @pl.loop(0, row_size + 1)
+        def _(k):
+            @pl.when(k < row_size)
+            def _():
+                base = (row + k + 1) % row_size * slab
+
+                @pl.loop(0, slab // tile)
+                def _(i):
+                    columns = pl.ds(pl.multiple_of(base + i * tile, tile), tile)
+                    lefts = left[:, :, columns].reshape(places * rows, tile)
+                    if g == 0:
+                        rights = latent[...].reshape(places * rows, 2 * half)
+                    else:
+                        rights = slope[...].reshape(places * rows, 2 * half).astype(bf16)
+                    product = lax.dot_general(
+                        lefts, rights, (((0,), (0,)), ((), ())), preferred_element_type=f32
+                    )
+                    at = pl.ds(pl.multiple_of(i * tile, tile), tile)
+                    acc[k % 2, at, :] = product[:, :half]
+                    near_out[g, k, at, :] = product[:, half:].astype(bf16)
+
+                near_copy(g, k).start()
+
+            @pl.when(k > 0)
+            def _():
+                near_copy(g, k - 1).wait_recv()
+                both = acc[(k - 1) % 2] + near_in[g, k - 1].astype(f32)
+
+                @pl.when(k < row_size)
+                def _():
+                    row_out[g, k - 1] = both.astype(bf16)
+                    row_copy(g, k - 1).start()
+
+                @pl.when(k == row_size)
+                def _():
+                    fin[g] = both
+
+    for g, out in enumerate((dec_grad_ref, enc_grad_ref)):
+        for k in range(row_size - 1):
+            row_copy(g, k).wait_recv()
+        out[...] = (
+            fin[g] + row_in[g, 0].astype(f32) + row_in[g, 1].astype(f32) + row_in[g, 2].astype(f32)
+        ).astype(bf16)
+
+    for copy in weights:
+        copy.wait_send()
+
+    @pl.loop(0, SUBS)
+    def _(s):
+        for way in (1, -1):
+            @pl.when(has_next(way))
+            def _():
+                x_copy(place, s, way, True).wait_send()
+                r_copy(place, s, way).wait_send()
+
+                @pl.loop(0, places)
+                def _(q):
+                    @pl.when((q - place) * way < 0)
+                    def _():
+                        x_copy(q, s, way, False).wait_send()
+                        r_copy(q, s, way).wait_send()
+
+                    @pl.when((q - place) * way > 0)
+                    def _():
+                        p_copy(q, s, way).wait_send()
+
+    for g in range(2):
+        for k in range(row_size):
+            near_copy(g, k).wait_send()
+        for k in range(row_size - 1):
+            row_copy(g, k).wait_send()
+
+
+def fused_on_device(activations, block_ids, enc_weight, enc_bias, dec_weight, dec_bias):
+    rows, features = activations.shape
+    half = enc_weight.shape[0]
+    places = lax.axis_size("dict") // 2
+    row_size = lax.axis_size("row")
+    slab = features // row_size
+    f32, bf16 = jnp.float32, jnp.bfloat16
+    shifted = (activations.astype(f32) - dec_bias[None, :]).astype(bf16)
+    active = jnp.any(
+        block_ids[:, :, None] == jnp.arange(128, dtype=jnp.int32)[None, None, :], axis=1
+    ).astype(bf16)
+    data = jnp.concatenate([shifted, active], axis=1)
+    bias = jnp.broadcast_to(enc_bias[None, :], (8, half))
+    dma = pltpu.SemaphoreType.DMA
+    rebuilt, enc_grad, dec_grad = pl.pallas_call(
+        step_kernel,
+        out_shape=(
+            jax.ShapeDtypeStruct((rows, features), bf16),
+            jax.ShapeDtypeStruct((slab, half), bf16),
+            jax.ShapeDtypeStruct((slab, half), bf16),
+        ),
+        in_specs=[pl.BlockSpec(memory_space=pltpu.VMEM)] * 6,
+        out_specs=[pl.BlockSpec(memory_space=pltpu.VMEM)] * 3,
+        scratch_shapes=[
+            pltpu.VMEM((places, rows, features + 128), bf16),
+            pltpu.VMEM((places, rows, features), bf16),
+            pltpu.VMEM((half, features), bf16),
+            pltpu.VMEM((half, features), bf16),
+            pltpu.VMEM((8, half), f32),
+            pltpu.VMEM((places, rows, features), bf16),
+            pltpu.VMEM((rows, features), f32),
+            pltpu.VMEM((2, places, rows, features), bf16),
+            pltpu.VMEM((places, rows, 2 * half), bf16),
+            pltpu.VMEM((places, rows, 2 * half), f32),
+            pltpu.VMEM((2, slab, half), f32),
+            pltpu.VMEM((2, slab, half), f32),
+            pltpu.VMEM((2, row_size, slab, half), bf16),
+            pltpu.VMEM((2, row_size, slab, half), bf16),
+            pltpu.VMEM((2, row_size - 1, slab, half), bf16),
+            pltpu.VMEM((2, row_size - 1, slab, half), bf16),
+            dma((3,)), dma((3,)),
+            dma((2, places, SUBS)), dma((places, SUBS)),
+            dma((places, SUBS)), dma((2, places, SUBS)),
+            dma((2, places, SUBS)), dma((places, SUBS)),
+            dma((2, row_size)), dma((2, row_size)),
+            dma((2, row_size - 1)), dma((2, row_size - 1)),
+        ],
+        compiler_params=pltpu.CompilerParams(
+            collective_id=0, has_side_effects=True, vmem_limit_bytes=67043328
+        ),
+    )(data, activations, bias, dec_bias[None, :], enc_weight, dec_weight)
+    return (rebuilt, enc_grad, dec_grad)
+
+
 def solution(mesh):
+    short_chain = mesh.shape["dict"] <= 8
     return jax.shard_map(
-        on_device,
+        fused_on_device if short_chain else on_device,
         mesh=mesh,
         in_specs=(
             P(("row", "dict"), None),

time: 627 us -> 269 us (0.43)
  blocking collectives: 289 us -> 0 us
  Pallas kernels: 0 us -> 260 us
  waiting for transfers between devices: 227 us -> 0 us
  local copies, waits for them, and re-layouts: 51.5 us -> 5.25 us
  matrix products: 19.2 us -> 0 us
  other arithmetic: 20.8 us -> 3.32 us
  between operations: 14.2 us -> 0.68 us
    all_to_all x2 -> x0, blocking collectives: 289 us -> none  [the longest x1 146 us: on_device(): lax.all_to_all(outgoing, 'dict', split_axis=0, concat_axis=0, tiled=True)]
    pallas_call x0 -> x1, Pallas kernels: none -> 260 us  [fused_on_device(): pl.pallas_call(step_kernel, out_shape=(jax.ShapeDtypeStruct((rows, featur...]
    all_to_all x1 -> x0, waiting for transfers between devices: 139 us -> none  [on_device(): lax.all_to_all(partial_value, 'dict', split_axis=0, concat_axis=0, tiled=...]
    reduce_scatter x2 -> x0, waiting for transfers between devices: 87.9 us -> none  [on_device(): lax.psum_scatter(product.reshape(features // row_size * lax.axis_size('ro...]
    gather x3 -> x0, local copies, waits for them, and re-layouts: 23.6 us -> none  [the longest x1 12.2 us: on_device(): returned.reshape(-1, features)[target].astype(jnp.float32)]
    dot_general x5 -> x0, matrix products: 19.2 us -> none  [the longest x1 6.17 us: on_device(): jnp.einsum('sbmc,sbmd->dbc', latent_grad, received, preferred_element_typ...]
    convert_element_type x2 -> x0, local copies, waits for them, and re-layouts: 11.4 us -> none  [the longest x1 8.33 us: on_device(): returned.reshape(-1, features)[target].astype(jnp.float32)]
    reshape x2 -> x0, local copies, waits for them, and re-layouts: 11.3 us -> none  [on_device(): product.reshape(features // row_size * lax.axis_size('row'), local_latents)]
  transfers between devices with their start and end apart: 3 -> 0, of which waited for: 3 -> 0; matrix products, arithmetic and copies ran while one was open for 3% -> 0% of each run, Pallas kernels for 0% -> 0%
where the time goes in v2:
time: 269 us
  Pallas kernels  260 us (97%)
  local copies, waits for them, and re-layouts  5.25 us (2%)
  other arithmetic  3.32 us (1%)
    pallas_call x1, Pallas kernels, fused_on_device(): pl.pallas_call(step_kernel, out_shape=(jax.ShapeDtypeStruct((rows, featur...  260 us

profile of v2, /device:TPU:0, one launch (start us, length us, event | category | flops | bytes accessed | tf_op | source)
XLA Modules:
  0.0 269.2 jit_solution(16995651062332454045)
XLA Ops:
  0.6 1.3 broadcast_in_dim.4.bias_ref
  1.9 0.8 fusion
  2.8 1.4 subtract_convert_fusion
  4.2 1.1 pad_maximum_fusion.x_ref
  5.3 260.0 %shard_map.85 = (bf16[128,4096]{1,0:T(8,128)(2,1)}, bf16[1024,256]{1,0:T(8,128)(2,1)}, bf16[1024,256]{1,0:T(8,128)(2,1)}) custom-call(bf16[128,4224]{1,0:T(8,128)(2,1)} %pad_maximum_fusion.x_ref, bf16[128,4096]{1,0:T(8,128)(2,1)} %act_ref.1, f32[8,256]{1,0:T(8,128)} %broadcast_in_dim.4.bias_ref, f32[1,4096]{1,0:T(1,128)} %bitcast.1, ...), custom_call_target="tpu_custom_call" | custom-call | tf_op jit(solution)/shard_map/pallas_call | solution.py:464
  265.2 0.0 copy-start.1
  265.2 0.0 copy-start
  265.3 2.4 copy.13
  267.6 0.0 copy-done.1
  267.6 0.8 copy.14
  268.4 0.0 copy-done
  268.4 0.8 copy.15
  (1 shorter events, 0.0 us)
Async XLA Ops:
  265.2 2.4 copy-start.1
  265.2 3.2 %copy-start = (bf16[1024,256]{1,0:T(8,128)(2,1)S(1)}, bf16[1024,256]{1,0:T(8,128)(2,1)}, u32[]{:S(2)}) copy-start(bf16[1024,256]{1,0:T(8,128)(2,1)} %get-tuple-element.8) | copy-start | bytes 1572868

commit v3 on v2

--- a/solution.py
+++ b/solution.py
@@ -260,33 +260,39 @@
 
     each_columns(keep_total)
 
-    @pl.loop(2, 2 * places)
-    def _(i):
-        way = 1 - 2 * (i % 2)
-        q = place - way * (i // 2)
-
-        @pl.when(jnp.logical_and(q >= 0, q < places))
-        def _():
-            @pl.loop(0, SUBS)
-            def _(s):
-                x_copy(q, s, way, False).wait_recv()
-
-                @pl.when(has_next(way))
+    @pl.loop(1, places)
+    def _(distance):
+        @pl.loop(0, SUBS)
+        def _(s):
+            for way in (1, -1):
+                @pl.when(has_next(-way * distance))
                 def _():
-                    x_copy(q, s, way, False).start()
-
-            forward(q)
-
-            def keep_part(columns):
-                part[q, :, columns] = decoded(q, columns).astype(bf16)
-
-            each_columns(keep_part)
-
-            @pl.when(jnp.logical_not(has_next(way)))
+                    q = place - way * distance
+                    x_copy(q, s, way, False).wait_recv()
+
+                    @pl.when(has_next(way))
+                    def _():
+                        x_copy(q, s, way, False).start()
+
+        @pl.loop(0, 2)
+        def _(turn):
+            way = 1 - 2 * turn
+            q = place - way * distance
+
+            @pl.when(jnp.logical_and(q >= 0, q < places))
             def _():
-                @pl.loop(0, SUBS)
-                def _(s):
-                    p_copy(q, s, -way).start()
+                forward(q)
+
+                def keep_part(columns):
+                    part[q, :, columns] = decoded(q, columns).astype(bf16)
+
+                each_columns(keep_part)
+
+                @pl.when(jnp.logical_not(has_next(way)))
+                def _():
+                    @pl.loop(0, SUBS)
+                    def _(s):
+                        p_copy(q, s, -way).start()
 
     def finish(s):
         here = part_rows(s)
@@ -343,22 +349,33 @@
 
     backward(place)
 
-    @pl.loop(2, 2 * places)
-    def _(i):
-        way = 1 - 2 * (i % 2)
-        q = place - way * (i // 2)
-
-        @pl.when(jnp.logical_and(q >= 0, q < places))
+    def take_residual(q, s):
+        way = jnp.where(q < place, 1, -1)
+        r_copy(q, s, way).wait_recv()
+
+        @pl.when(has_next(way))
         def _():
-            @pl.loop(0, SUBS)
-            def _(s):
-                r_copy(q, s, way).wait_recv()
-
-                @pl.when(has_next(way))
-                def _():
-                    r_copy(q, s, way).start()
-
-            backward(q)
+            r_copy(q, s, way).start()
+
+    low = place < places // 2
+    first = jnp.where(low, place + 1, place - 1)
+    second = jnp.where(low, 2 - 2 * place, 7 - 2 * place)
+    third = jnp.where(low, 3, 0)
+
+    @pl.loop(0, SUBS)
+    def _(s):
+        take_residual(first, s)
+
+    backward(first)
+
+    @pl.loop(0, SUBS)
+    def _(s):
+        take_residual(second, s)
+        take_residual(third, s)
+
+    @pl.loop(0, 2)
+    def _(turn):
+        backward(jnp.where(turn == 0, second, third))
 
     tile = 256
 
@@ -502,7 +519,7 @@
 
 
 def solution(mesh):
-    short_chain = mesh.shape["dict"] <= 8
+    short_chain = mesh.shape["dict"] == 8 and mesh.shape["row"] == 4
     return jax.shard_map(
         fused_on_device if short_chain else on_device,
         mesh=mesh,

time: 269 us -> 262 us (0.974)
  Pallas kernels: 260 us -> 252 us
    pallas_call x1, Pallas kernels: 260 us -> 252 us  [fused_on_device(): pl.pallas_call(step_kernel, out_shape=(jax.ShapeDtypeStruct((rows, featur...]
where the time goes in v3:
time: 262 us; the launch traced here: 261 us
  Pallas kernels  252 us (96%)
  local copies, waits for them, and re-layouts  5.25 us (2%)
  other arithmetic  3.32 us (1%)
    pallas_call x1, Pallas kernels, fused_on_device(): pl.pallas_call(step_kernel, out_shape=(jax.ShapeDtypeStruct((rows, featur...  252 us

profile of v3, /device:TPU:0, one launch (start us, length us, event | category | flops | bytes accessed | tf_op | source)
XLA Modules:
  0.0 261.5 jit_solution(17395802880471880301)
XLA Ops:
  0.6 1.3 broadcast_in_dim.4.bias_ref
  1.9 0.8 fusion
  2.8 1.4 subtract_convert_fusion
  4.2 1.1 pad_maximum_fusion.x_ref
  5.3 252.2 %shard_map.85 = (bf16[128,4096]{1,0:T(8,128)(2,1)}, bf16[1024,256]{1,0:T(8,128)(2,1)}, bf16[1024,256]{1,0:T(8,128)(2,1)}) custom-call(bf16[128,4224]{1,0:T(8,128)(2,1)} %pad_maximum_fusion.x_ref, bf16[128,4096]{1,0:T(8,128)(2,1)} %act_ref.1, f32[8,256]{1,0:T(8,128)} %broadcast_in_dim.4.bias_ref, f32[1,4096]{1,0:T(1,128)} %bitcast.1, ...), custom_call_target="tpu_custom_call" | custom-call | tf_op jit(solution)/shard_map/pallas_call | solution.py:481
  257.5 0.0 copy-start.1
  257.5 0.0 copy-start
  257.5 2.4 copy.13
  259.9 0.0 copy-done.1
  259.9 0.8 copy.14
  260.7 0.0 copy-done
  260.7 0.8 copy.15
  (1 shorter events, 0.0 us)
Async XLA Ops:
  257.5 2.4 copy-start.1
  257.5 3.2 %copy-start = (bf16[1024,256]{1,0:T(8,128)(2,1)S(1)}, bf16[1024,256]{1,0:T(8,128)(2,1)}, u32[]{:S(2)}) copy-start(bf16[1024,256]{1,0:T(8,128)(2,1)} %get-tuple-element.8) | copy-start | bytes 1572868

commit v4 on v3

--- a/solution.py
+++ b/solution.py
@@ -304,40 +304,42 @@
             def _():
                 r_copy(place, s, way).start()
 
-    @pl.loop(0, 2)
-    def _(turn):
-        low = jnp.where(place < places // 2, 1, -1)
-        way = low * (1 - 2 * turn)
-        lane = (way + 1) // 2
-
-        @pl.when(has_next(-way))
-        def _():
-            @pl.loop(0, places)
-            def _(t):
-                q = place + way * t
-
-                @pl.when(jnp.logical_and(q >= 0, q < places))
-                def _():
-                    @pl.loop(0, SUBS)
-                    def _(s):
-                        here = part_rows(s)
-                        p_copy(q, s, way).wait_recv()
-
-                        @pl.when(t == 0)
-                        def _():
-                            total[here, :] += incoming[lane, q, here, :].astype(f32)
-
-                            @pl.when(turn == 1)
-                            def _():
-                                finish(s)
-
-                        @pl.when(t > 0)
-                        def _():
-                            part[q, here, :] = (
-                                part[q, here, :].astype(f32)
-                                + incoming[lane, q, here, :].astype(f32)
-                            ).astype(bf16)
-                            p_copy(q, s, way).start()
+    ahead = jnp.where(place < places // 2, 1, -1)
+
+    def add_own(s, way):
+        here = part_rows(s)
+        p_copy(place, s, way).wait_recv()
+        total[here, :] += incoming[(way + 1) // 2, place, here, :].astype(f32)
+
+    def pass_on(q, s, way):
+        here = part_rows(s)
+        p_copy(q, s, way).wait_recv()
+        part[q, here, :] = (
+            part[q, here, :].astype(f32) + incoming[(way + 1) // 2, q, here, :].astype(f32)
+        ).astype(bf16)
+        p_copy(q, s, way).start()
+
+    @pl.when(inside)
+    def _():
+        @pl.loop(0, SUBS)
+        def _(s):
+            add_own(s, ahead)
+
+        @pl.loop(0, SUBS)
+        def _(s):
+            pass_on(place + ahead, s, ahead)
+
+    @pl.loop(0, SUBS)
+    def _(s):
+        add_own(s, -ahead)
+        finish(s)
+
+    @pl.when(inside)
+    def _():
+        @pl.loop(0, SUBS)
+        def _(s):
+            pass_on(place + 2 * ahead, s, ahead)
+            pass_on(place - ahead, s, -ahead)
 
     def backward(q):
         for h, weight in enumerate((dec_ref, dec_far)):

time: 262 us -> 257 us (0.981)
  Pallas kernels: 252 us -> 248 us
    pallas_call x1, Pallas kernels: 252 us -> 248 us  [fused_on_device(): pl.pallas_call(step_kernel, out_shape=(jax.ShapeDtypeStruct((rows, featur...]
where the time goes in v4:
time: 257 us
  Pallas kernels  248 us (96%)
  local copies, waits for them, and re-layouts  5.25 us (2%)
  other arithmetic  3.32 us (1%)
    pallas_call x1, Pallas kernels, fused_on_device(): pl.pallas_call(step_kernel, out_shape=(jax.ShapeDtypeStruct((rows, featur...  248 us

profile of v4, /device:TPU:0, one launch (start us, length us, event | category | flops | bytes accessed | tf_op | source)
XLA Modules:
  0.0 257.1 jit_solution(8433289188057385099)
XLA Ops:
  0.6 1.3 broadcast_in_dim.4.bias_ref
  1.9 0.8 fusion
  2.8 1.4 subtract_convert_fusion
  4.2 1.1 pad_maximum_fusion.x_ref
  5.3 247.9 %shard_map.85 = (bf16[128,4096]{1,0:T(8,128)(2,1)}, bf16[1024,256]{1,0:T(8,128)(2,1)}, bf16[1024,256]{1,0:T(8,128)(2,1)}) custom-call(bf16[128,4224]{1,0:T(8,128)(2,1)} %pad_maximum_fusion.x_ref, bf16[128,4096]{1,0:T(8,128)(2,1)} %act_ref.1, f32[8,256]{1,0:T(8,128)} %broadcast_in_dim.4.bias_ref, f32[1,4096]{1,0:T(1,128)} %bitcast.1, ...), custom_call_target="tpu_custom_call" | custom-call | tf_op jit(solution)/shard_map/pallas_call | solution.py:483
  253.2 0.0 copy-start.1
  253.2 0.0 copy-start
  253.2 2.4 copy.13
  255.5 0.0 copy-done.1
  255.6 0.8 copy.14
  256.3 0.0 copy-done
  256.3 0.8 copy.15
  (1 shorter events, 0.0 us)
Async XLA Ops:
  253.2 2.4 copy-start.1
  253.2 3.2 %copy-start = (bf16[1024,256]{1,0:T(8,128)(2,1)S(1)}, bf16[1024,256]{1,0:T(8,128)(2,1)}, u32[]{:S(2)}) copy-start(bf16[1024,256]{1,0:T(8,128)(2,1)} %get-tuple-element.8) | copy-start | bytes 1572868

commit v5 on v4

--- a/solution.py
+++ b/solution.py
@@ -219,7 +219,22 @@
     ]
     for copy in weights:
         copy.start()
+    def relay(distance):
+        @pl.loop(0, SUBS)
+        def _(s):
+            for way in (1, -1):
+                @pl.when(has_next(-way * distance))
+                def _():
+                    q = place - way * distance
+                    x_copy(q, s, way, False).wait_recv()
+
+                    @pl.when(has_next(way))
+                    def _():
+                        x_copy(q, s, way, False).start()
+
     held[place] = x_ref[...]
+    relay(1)
+
     for copy in weights:
         copy.wait_recv()
 
@@ -262,17 +277,9 @@
 
     @pl.loop(1, places)
     def _(distance):
-        @pl.loop(0, SUBS)
-        def _(s):
-            for way in (1, -1):
-                @pl.when(has_next(-way * distance))
-                def _():
-                    q = place - way * distance
-                    x_copy(q, s, way, False).wait_recv()
-
-                    @pl.when(has_next(way))
-                    def _():
-                        x_copy(q, s, way, False).start()
+        @pl.when(distance > 1)
+        def _():
+            relay(distance)
 
         @pl.loop(0, 2)
         def _(turn):
@@ -349,8 +356,6 @@
             )
             slope[q, :, span] = slope[q, :, span] * up
 
-    backward(place)
-
     def take_residual(q, s):
         way = jnp.where(q < place, 1, -1)
         r_copy(q, s, way).wait_recv()
@@ -368,6 +373,7 @@
     def _(s):
         take_residual(first, s)
 
+    backward(place)
     backward(first)
 
     @pl.loop(0, SUBS)

time: 257 us -> 256 us (level)
  no operation moved by 1% of the time
where the time goes in v5:
time: 256 us
  Pallas kernels  247 us (96%)
  local copies, waits for them, and re-layouts  5.25 us (2%)
  other arithmetic  3.32 us (1%)
    pallas_call x1, Pallas kernels, fused_on_device(): pl.pallas_call(step_kernel, out_shape=(jax.ShapeDtypeStruct((rows, featur...  247 us

profile of v5, /device:TPU:0, one launch (start us, length us, event | category | flops | bytes accessed | tf_op | source)
XLA Modules:
  0.0 255.9 jit_solution(8849717905149913449)
XLA Ops:
  0.6 1.3 broadcast_in_dim.4.bias_ref
  1.9 0.8 fusion
  2.8 1.4 subtract_convert_fusion
  4.2 1.1 pad_maximum_fusion.x_ref
  5.3 246.7 %shard_map.85 = (bf16[128,4096]{1,0:T(8,128)(2,1)}, bf16[1024,256]{1,0:T(8,128)(2,1)}, bf16[1024,256]{1,0:T(8,128)(2,1)}) custom-call(bf16[128,4224]{1,0:T(8,128)(2,1)} %pad_maximum_fusion.x_ref, bf16[128,4096]{1,0:T(8,128)(2,1)} %act_ref.1, f32[8,256]{1,0:T(8,128)} %broadcast_in_dim.4.bias_ref, f32[1,4096]{1,0:T(1,128)} %bitcast.1, ...), custom_call_target="tpu_custom_call" | custom-call | tf_op jit(solution)/shard_map/pallas_call | solution.py:489
  251.9 0.0 copy-start.1
  252.0 0.0 copy-start
  252.0 2.4 copy.13
  254.3 0.0 copy-done.1
  254.3 0.8 copy.14
  255.1 0.0 copy-done
  255.1 0.8 copy.15
  (1 shorter events, 0.0 us)
Async XLA Ops:
  251.9 2.4 copy-start.1
  252.0 3.2 %copy-start = (bf16[1024,256]{1,0:T(8,128)(2,1)S(1)}, bf16[1024,256]{1,0:T(8,128)(2,1)}, u32[]{:S(2)}) copy-start(bf16[1024,256]{1,0:T(8,128)(2,1)} %get-tuple-element.8) | copy-start | bytes 1572868
